TPU v7x, 128 devices: a whole 4x4x4 slice. The times are simulated.
128 devices in a mesh: grp: 8 (over y, core), dev: 16 (over z, x).
Axes of the slice: x: 4, y: 4, z: 4, core: 2. Of those that a mesh axis runs over, the one named last changes fastest.
Arguments:
- basis_old: float32 [128, 2097152], P(None, ('grp', 'dev')), as said below
- values_old: float32 [128], replicated, may hold values from 1 to 4
- snapshots: float32 [2, 64, 2097152], P(None, None, ('grp', 'dev'))
- wet_counts: int32 [128], P(('grp', 'dev')), may hold values from 1 to 128, as said below
Outputs:
- basis_new: float32 [128, 2097152], P(None, ('grp', 'dev'))
- values_new: float32 [128], replicated
Inputs may be any that keep to these rules, and one draw needn't show every extreme that they name: `wet_counts`: every device has at least one wet block, and some device has all 128 blocks wet. basis_old is zero on every cell that wet_mask marks dry.
All inputs are finite; a program needn't handle non-finite values.
Results may differ from a plain program's by a relative error of at most 0.0003.
Values sent between devices are 32-bit elements; how exact they have to be, the bound alone decides.
No kernel may reach another device: no remote copies, remote signals or barrier semaphores. Data moves between devices by JAX's collectives and lax.ppermute only.
A program may use at most 128 MiB of HBM per device.

v0:
```python
import jax
import jax.numpy as jnp
from jax import lax
from jax.sharding import PartitionSpec as P

BLOCK = 128
SWEEPS = 3


def matmul_nn(left_op, right_op):
    return jnp.dot(
        left_op, right_op, precision=lax.Precision.HIGHEST, preferred_element_type=jnp.float32
    )


def matmul_nt(left_op, right_op):
    return lax.dot_general(
        left_op,
        right_op,
        (((1,), (1,)), ((), ())),
        precision=lax.Precision.HIGHEST,
        preferred_element_type=jnp.float32,
    )


def matmul_tn(left_op, right_op):
    return lax.dot_general(
        left_op,
        right_op,
        (((0,), (0,)), ((), ())),
        precision=lax.Precision.HIGHEST,
        preferred_element_type=jnp.float32,
    )


def assemble(values, project, factor):
    upper_block = jnp.concatenate([jnp.diag(values), project], 1)
    bottom = jnp.concatenate(
        [jnp.zeros((factor.shape[0], values.shape[0]), jnp.float32), factor.T], 1
    )
    return jnp.concatenate([upper_block, bottom], 0)


def refine(core_matrix, rank_width):
    frame_now = jnp.eye(core_matrix.shape[0], rank_width, dtype=jnp.float32)
    for repeat in range(SWEEPS):
        grown_cols = matmul_nn(core_matrix, matmul_tn(core_matrix, frame_now))
        lower_part = jnp.linalg.cholesky(matmul_tn(grown_cols, grown_cols))
        frame_now = jax.scipy.linalg.solve_triangular(lower_part, grown_cols.T, lower=True).T
    return frame_now


def per_device(basis_old, values_old, snapshots, wet_counts):
    counts = lax.all_gather(wet_counts, ("grp", "dev"), axis=0, tiled=True)
    wet_total = jnp.sum(counts).astype(jnp.float32) * BLOCK
    rows_here = basis_old.shape[1]
    wet_mask = (lax.iota(jnp.int32, rows_here) // BLOCK < wet_counts[0]).astype(jnp.float32)
    rank_width = basis_old.shape[0]

    def update_one(state_pair, snapshot):
        current, values = state_pair
        columns = snapshot * wet_mask[None, :]
        project = lax.psum(matmul_nt(current, columns), ("grp", "dev")) / wet_total
        remainder = columns - matmul_tn(project, current)
        gram = lax.psum(matmul_nt(remainder, remainder), ("grp", "dev")) / wet_total
        factor = jnp.linalg.cholesky(gram)
        fresh_rows = jax.scipy.linalg.solve_triangular(factor, remainder, lower=True)
        core_matrix = assemble(values, project, factor)
        frame_now = refine(core_matrix, rank_width)
        stacked = jnp.concatenate([current, fresh_rows], 0)
        new_basis = matmul_tn(frame_now, stacked)
        rotated = matmul_tn(frame_now, core_matrix)
        new_values = jnp.sqrt(jnp.sum(rotated * rotated, axis=1))
        return ((new_basis, new_values), None)

    (current, values), _ = lax.scan(update_one, (basis_old, values_old), snapshots)
    return (current, values)


def solution(mesh):
    return jax.shard_map(
        per_device,
        mesh=mesh,
        in_specs=(P(None, ("grp", "dev")), P(), P(None, None, ("grp", "dev")), P(("grp", "dev"))),
        out_specs=(P(None, ("grp", "dev")), P()),
        check_vma=False,
    )
```

profile of v0, /device:TPU:1, one launch (start us, length us, event | category | flops | bytes accessed | tf_op | source)
XLA Modules:
  0.0 607.9 jit_solution(14972124603921048518)
XLA Ops:
  0.6 7.6 %copy.42 = f32[128,16384]{1,0:T(8,128)} copy(f32[128,16384]{1,0:T(8,128)} %param.9) | data formatting | bytes 16777216
  9.0 68.6 %all-reduce.1 = s32[128]{0:T(128)S(1)} all-reduce(s32[128]{0:T(128)S(1)} %dynamic-update-slice.5), channel_id=1, replica_groups=mesh['grp'=8,'dev'=16] {'grp','dev'}, use_global_device_ids=true, to_apply=%add.1 | all-reduce | flops 128 | bytes 1024
  79.0 527.8 %while.13 = (s32[]{:T(128)}, f32[128,16384]{1,0:T(8,128)}, f32[128]{0:T(128)S(1)}, f32[2,64,16384]{2,1,0:T(8,128)}, f32[]{:T(128)}, /*index=5*/s32[]{:T(128)}, s32[]{:T(128)}) while((s32[]{:T(128)}, f32[128,16384]{1,0:T(8,128)}, f32[128]{0:T(128)S(1)}, f32[2,64,16384]{2,1,0:T(8,128)}, f32[]{:T(128)}, /*index=5*/s32[]{:T(128)}, ...), condition=%wide.region_9.12_spmd.clone, body=%wide.region_1.11_spmd.clone.sunk | while | flops 10294632448 | bytes 169318064 | solution.py:76
  79.3 3.5 copy.45
  88.1 8.8 %fusion.153 = f32[128,64]{0,1:T(8,128)S(1)} fusion(f32[128,16384]{1,0:T(8,128)S(1)} %copy.45, f32[2,64,16384]{2,1,0:T(8,128)S(1)} %copy-done.2, s32[]{:T(128)} %get-tuple-element.116, f32[16384]{0:T(1024)S(1)} %fusion.152), kind=kOutput, calls=%fused_computation.11.clone.1 | convolution fusion | flops 1611661312 | bytes 12681220 | tf_op jit(solution)/shard_map/while/body/eval_jaxpr/dot_general | solution.py:17
  96.9 62.9 %psum.18 = f32[128,64]{0,1:T(8,128)S(1)} all-reduce(f32[128,64]{0,1:T(8,128)S(1)} %fusion.153), channel_id=1, replica_groups=mesh['grp'=8,'dev'=16] {'grp','dev'}, use_global_device_ids=true, to_apply=%region_2.2 | all-reduce | flops 8192 | bytes 65536 | tf_op jit(solution)/shard_map/while/body/eval_jaxpr/psum | solution.py:63
  159.8 7.8 %convolution_subtract_fusion.2 = f32[64,16384]{1,0:T(8,128)S(1)} fusion(f32[128,64]{0,1:T(8,128)S(1)} %broadcast_divide_fusion.4, f32[128,16384]{1,0:T(8,128)} %copy-done, f32[2,64,16384]{2,1,0:T(8,128)} %get-tuple-element.126, s32[]{:T(128)} %get-tuple-element.116, f32[16384]{0:T(1024)S(1)} %fusion.152), kind=kOutput, calls=%fused_computation.1.clone.1 | convolution fusion | flops 1612709888 | bytes 16875524 | tf_op jit(solution)/shard_map/while/body/eval_jaxpr/dot_general | solution.py:27
  173.0 64.8 %psum.19 = f32[64,64]{0,1:T(8,128)S(1)} all-reduce(f32[64,64]{0,1:T(8,128)S(1)} %fusion.154), channel_id=1, replica_groups=mesh['grp'=8,'dev'=16] {'grp','dev'}, use_global_device_ids=true, to_apply=%region_3.3 | all-reduce | flops 4096 | bytes 32768 | tf_op jit(solution)/shard_map/while/body/eval_jaxpr/psum | solution.py:65
  238.0 5.8 cholesky.285
  246.7 11.7 %cholesky.286 = f32[128,128]{1,0:T(8,128)S(1)} custom-call(f32[128,128]{1,0:T(8,128)S(1)} %fusion.160), custom_call_target="Cholesky" | custom-call | tf_op jit(solution)/shard_map/while/body/eval_jaxpr/jit(cholesky)/cholesky | solution.py:48
  259.7 9.8 %custom-call.22 = f32[1,128,128]{1,2,0:T(8,128)S(1)} custom-call(f32[1,128,128]{2,1,0:T(8,128)S(1)} %fusion.162), custom_call_target="InvertDiagBlocksLowerTriangular" | custom-call | tf_op jit(solution)/shard_map/while/body/eval_jaxpr/jit(_solve_triangular)/triangular_solve | solution.py:49
  271.3 11.9 %cholesky.287 = f32[128,128]{1,0:T(8,128)S(1)} custom-call(f32[128,128]{1,0:T(8,128)S(1)} %fusion.167), custom_call_target="Cholesky" | custom-call | tf_op jit(solution)/shard_map/while/body/eval_jaxpr/jit(cholesky)/cholesky | solution.py:48
  284.5 9.8 %custom-call.23 = f32[1,128,128]{1,2,0:T(8,128)S(1)} custom-call(f32[1,128,128]{2,1,0:T(8,128)S(1)} %fusion.169), custom_call_target="InvertDiagBlocksLowerTriangular" | custom-call | tf_op jit(solution)/shard_map/while/body/eval_jaxpr/jit(_solve_triangular)/triangular_solve | solution.py:49
  296.0 11.7 %cholesky.288 = f32[128,128]{1,0:T(8,128)S(1)} custom-call(f32[128,128]{1,0:T(8,128)S(1)} %fusion.174), custom_call_target="Cholesky" | custom-call | tf_op jit(solution)/shard_map/while/body/eval_jaxpr/jit(cholesky)/cholesky | solution.py:48
  309.1 9.8 %custom-call.24 = f32[1,128,128]{1,2,0:T(8,128)S(1)} custom-call(f32[1,128,128]{2,1,0:T(8,128)S(1)} %fusion.175), custom_call_target="InvertDiagBlocksLowerTriangular" | custom-call | tf_op jit(solution)/shard_map/while/body/eval_jaxpr/jit(_solve_triangular)/triangular_solve | solution.py:49
  319.7 4.9 custom-call.25
  324.6 5.6 fusion.177
  330.2 12.3 %fusion.178 = f32[128,16384]{1,0:T(8,128)} fusion(f32[128,192]{0,1:T(8,128)S(1)} %fusion.176, f32[64,16384]{1,0:T(8,128)S(1)} %fusion.177, f32[128,16384]{1,0:T(8,128)} %copy-done), kind=kOutput, calls=%fused_computation.2.clone.1 | convolution fusion | flops 4834983936 | bytes 21069824 | tf_op jit(solution)/shard_map/while/body/eval_jaxpr/dot_general | solution.py:27
  351.6 8.8 %fusion.153 = f32[128,64]{0,1:T(8,128)S(1)} fusion(f32[128,16384]{1,0:T(8,128)S(1)} %copy.45, f32[2,64,16384]{2,1,0:T(8,128)S(1)} %copy-done.2, s32[]{:T(128)} %get-tuple-element.116, f32[16384]{0:T(1024)S(1)} %fusion.152), kind=kOutput, calls=%fused_computation.11.clone.1 | convolution fusion | flops 1611661312 | bytes 12681220 | tf_op jit(solution)/shard_map/while/body/eval_jaxpr/dot_general | solution.py:17
  360.4 63.0 %psum.18 = f32[128,64]{0,1:T(8,128)S(1)} all-reduce(f32[128,64]{0,1:T(8,128)S(1)} %fusion.153), channel_id=1, replica_groups=mesh['grp'=8,'dev'=16] {'grp','dev'}, use_global_device_ids=true, to_apply=%region_2.2 | all-reduce | flops 8192 | bytes 65536 | tf_op jit(solution)/shard_map/while/body/eval_jaxpr/psum | solution.py:63
  423.4 7.8 %convolution_subtract_fusion.2 = f32[64,16384]{1,0:T(8,128)S(1)} fusion(f32[128,64]{0,1:T(8,128)S(1)} %broadcast_divide_fusion.4, f32[128,16384]{1,0:T(8,128)} %copy-done, f32[2,64,16384]{2,1,0:T(8,128)} %get-tuple-element.126, s32[]{:T(128)} %get-tuple-element.116, f32[16384]{0:T(1024)S(1)} %fusion.152), kind=kOutput, calls=%fused_computation.1.clone.1 | convolution fusion | flops 1612709888 | bytes 16875524 | tf_op jit(solution)/shard_map/while/body/eval_jaxpr/dot_general | solution.py:27
  436.6 64.4 %psum.19 = f32[64,64]{0,1:T(8,128)S(1)} all-reduce(f32[64,64]{0,1:T(8,128)S(1)} %fusion.154), channel_id=1, replica_groups=mesh['grp'=8,'dev'=16] {'grp','dev'}, use_global_device_ids=true, to_apply=%region_3.3 | all-reduce | flops 4096 | bytes 32768 | tf_op jit(solution)/shard_map/while/body/eval_jaxpr/psum | solution.py:65
  501.1 5.8 cholesky.285
  509.8 11.7 %cholesky.286 = f32[128,128]{1,0:T(8,128)S(1)} custom-call(f32[128,128]{1,0:T(8,128)S(1)} %fusion.160), custom_call_target="Cholesky" | custom-call | tf_op jit(solution)/shard_map/while/body/eval_jaxpr/jit(cholesky)/cholesky | solution.py:48
  522.8 9.8 %custom-call.22 = f32[1,128,128]{1,2,0:T(8,128)S(1)} custom-call(f32[1,128,128]{2,1,0:T(8,128)S(1)} %fusion.162), custom_call_target="InvertDiagBlocksLowerTriangular" | custom-call | tf_op jit(solution)/shard_map/while/body/eval_jaxpr/jit(_solve_triangular)/triangular_solve | solution.py:49
  534.4 11.9 %cholesky.287 = f32[128,128]{1,0:T(8,128)S(1)} custom-call(f32[128,128]{1,0:T(8,128)S(1)} %fusion.167), custom_call_target="Cholesky" | custom-call | tf_op jit(solution)/shard_map/while/body/eval_jaxpr/jit(cholesky)/cholesky | solution.py:48
  547.6 9.8 %custom-call.23 = f32[1,128,128]{1,2,0:T(8,128)S(1)} custom-call(f32[1,128,128]{2,1,0:T(8,128)S(1)} %fusion.169), custom_call_target="InvertDiagBlocksLowerTriangular" | custom-call | tf_op jit(solution)/shard_map/while/body/eval_jaxpr/jit(_solve_triangular)/triangular_solve | solution.py:49
  559.2 11.7 %cholesky.288 = f32[128,128]{1,0:T(8,128)S(1)} custom-call(f32[128,128]{1,0:T(8,128)S(1)} %fusion.174), custom_call_target="Cholesky" | custom-call | tf_op jit(solution)/shard_map/while/body/eval_jaxpr/jit(cholesky)/cholesky | solution.py:48
  572.3 9.8 %custom-call.24 = f32[1,128,128]{1,2,0:T(8,128)S(1)} custom-call(f32[1,128,128]{2,1,0:T(8,128)S(1)} %fusion.175), custom_call_target="InvertDiagBlocksLowerTriangular" | custom-call | tf_op jit(solution)/shard_map/while/body/eval_jaxpr/jit(_solve_triangular)/triangular_solve | solution.py:49
  582.8 4.9 custom-call.25
  587.7 5.8 fusion.177
  593.6 12.3 %fusion.178 = f32[128,16384]{1,0:T(8,128)} fusion(f32[128,192]{0,1:T(8,128)S(1)} %fusion.176, f32[64,16384]{1,0:T(8,128)S(1)} %fusion.177, f32[128,16384]{1,0:T(8,128)} %copy-done), kind=kOutput, calls=%fused_computation.2.clone.1 | convolution fusion | flops 4834983936 | bytes 21069824 | tf_op jit(solution)/shard_map/while/body/eval_jaxpr/dot_general | solution.py:27
  (102 shorter events, 48.2 us)
Async XLA Ops:
  0.6 78.4 %copy-start.4 = (f32[128]{0:T(128)S(1)}, f32[128]{0:T(128)}, u32[]{:S(2)}) copy-start(f32[128]{0:T(128)} %param.10) | copy-start | bytes 1540
  79.3 8.8 %copy-start.2 = (f32[2,64,16384]{2,1,0:T(8,128)S(1)}, f32[2,64,16384]{2,1,0:T(8,128)}, u32[]{:S(2)}) copy-start(f32[2,64,16384]{2,1,0:T(8,128)} %get-tuple-element.126) | copy-start | bytes 25165828 | tf_op jit(solution)/shard_map/while
  82.8 4.3 copy-start
  167.6 2.0 copy-start.1
  342.8 8.8 %copy-start.2 = (f32[2,64,16384]{2,1,0:T(8,128)S(1)}, f32[2,64,16384]{2,1,0:T(8,128)}, u32[]{:S(2)}) copy-start(f32[2,64,16384]{2,1,0:T(8,128)} %get-tuple-element.126) | copy-start | bytes 25165828 | tf_op jit(solution)/shard_map/while
  346.3 4.3 copy-start
  431.2 2.0 copy-start.1
  606.9 0.5 copy-start.3
where the time goes:
time: 611 us; the launch traced here: 608 us
  blocking collectives  324 us (53%)
  other arithmetic  166 us (27%)
  matrix products  86 us (14%)
  local copies, waits for them, and re-layouts  27.7 us (5%)
    psum x2, blocking collectives, update_one(): gram = lax.psum(matmul_nt(remainder, remainder), ('grp', 'dev')) / wet_total  129 us
    psum x2, blocking collectives, update_one(): project = lax.psum(matmul_nt(current, columns), ('grp', 'dev')) / wet_total  126 us
    another operation x18, other arithmetic, refine(): lower_part = jnp.linalg.cholesky(matmul_tn(grown_cols, grown_cols))  74.8 us
    unnamed x1, blocking collectives  68.6 us
    another operation x12, other arithmetic, refine(): jax.scipy.linalg.solve_triangular(lower_part, grown_cols.T, lower=True)  62.7 us
    dot_general x18, matrix products, matmul_tn(): lax.dot_general(left_op, right_op, (((0,), (0,)), ((), ())), precision=la...  46.3 us
    dot_general x4, matrix products, matmul_nt(): lax.dot_general(left_op, right_op, (((1,), (1,)), ((), ())), precision=la...  24.4 us
    while x16, local copies, waits for them, and re-layouts  18.6 us

commit v1 on v0

--- a/solution.py
+++ b/solution.py
@@ -62,7 +62,7 @@
         columns = snapshot * wet_mask[None, :]
         project = lax.psum(matmul_nt(current, columns), ("grp", "dev")) / wet_total
         remainder = columns - matmul_tn(project, current)
-        gram = lax.psum(matmul_nt(remainder, remainder), ("grp", "dev")) / wet_total
+        gram = lax.psum(lax.psum(matmul_nt(remainder, remainder), "grp"), "dev") / wet_total
         factor = jnp.linalg.cholesky(gram)
         fresh_rows = jax.scipy.linalg.solve_triangular(factor, remainder, lower=True)
         core_matrix = assemble(values, project, factor)

time: 611 us -> 673 us (1.10)
  the two profiles are of different devices: /device:TPU:1 before, /device:TPU:0 now
where the time goes in v1:
time: 673 us; the launch traced here: 670 us
  blocking collectives  386 us (57%)
  other arithmetic  166 us (25%)
  matrix products  86.1 us (13%)
  local copies, waits for them, and re-layouts  27.7 us (4%)
    psum x2, blocking collectives, update_one(): lax.psum(lax.psum(matmul_nt(remainder, remainder), 'grp'), 'dev')  143 us
    psum x2, blocking collectives, update_one(): project = lax.psum(matmul_nt(current, columns), ('grp', 'dev')) / wet_total  126 us
    another operation x18, other arithmetic, refine(): lower_part = jnp.linalg.cholesky(matmul_tn(grown_cols, grown_cols))  74.8 us
    unnamed x1, blocking collectives  68.2 us
    another operation x12, other arithmetic, refine(): jax.scipy.linalg.solve_triangular(lower_part, grown_cols.T, lower=True)  62.7 us
    psum x2, blocking collectives, update_one(): lax.psum(matmul_nt(remainder, remainder), 'grp')  48.9 us
    dot_general x18, matrix products, matmul_tn(): lax.dot_general(left_op, right_op, (((0,), (0,)), ((), ())), precision=la...  46.4 us
    dot_general x4, matrix products, matmul_nt(): lax.dot_general(left_op, right_op, (((1,), (1,)), ((), ())), precision=la...  24.4 us

profile of v1, /device:TPU:0, one launch (start us, length us, event | category | flops | bytes accessed | tf_op | source)
XLA Modules:
  0.0 670.1 jit_solution(5607160687362473600)
XLA Ops:
  0.6 7.6 %copy.42 = f32[128,16384]{1,0:T(8,128)} copy(f32[128,16384]{1,0:T(8,128)} %param.9) | data formatting | bytes 16777216
  9.0 68.2 %all-reduce.1 = s32[128]{0:T(128)S(1)} all-reduce(s32[128]{0:T(128)S(1)} %dynamic-update-slice.5), channel_id=1, replica_groups=mesh['grp'=8,'dev'=16] {'grp','dev'}, use_global_device_ids=true, to_apply=%add.1 | all-reduce | flops 128 | bytes 1024
  78.6 590.4 %while.13 = (s32[]{:T(128)}, f32[128,16384]{1,0:T(8,128)}, f32[128]{0:T(128)S(1)}, f32[2,64,16384]{2,1,0:T(8,128)}, f32[]{:T(128)}, /*index=5*/s32[]{:T(128)}, s32[]{:T(128)}) while((s32[]{:T(128)}, f32[128,16384]{1,0:T(8,128)}, f32[128]{0:T(128)S(1)}, f32[2,64,16384]{2,1,0:T(8,128)}, f32[]{:T(128)}, /*index=5*/s32[]{:T(128)}, ...), condition=%wide.region_10.13_spmd.clone, body=%wide.region_1.12_spmd.clone.sunk | while | flops 10294636544 | bytes 169350832 | solution.py:76
  87.6 8.8 %fusion.153 = f32[128,64]{0,1:T(8,128)S(1)} fusion(f32[128,16384]{1,0:T(8,128)S(1)} %copy.45, f32[2,64,16384]{2,1,0:T(8,128)S(1)} %copy-done.2, s32[]{:T(128)} %get-tuple-element.116, f32[16384]{0:T(1024)S(1)} %fusion.152), kind=kOutput, calls=%fused_computation.11.clone.1 | convolution fusion | flops 1611661312 | bytes 12681220 | tf_op jit(solution)/shard_map/while/body/eval_jaxpr/dot_general | solution.py:17
  96.4 62.6 %psum.27 = f32[128,64]{0,1:T(8,128)S(1)} all-reduce(f32[128,64]{0,1:T(8,128)S(1)} %fusion.153), channel_id=1, replica_groups=mesh['grp'=8,'dev'=16] {'grp','dev'}, use_global_device_ids=true, to_apply=%region_2.2 | all-reduce | flops 8192 | bytes 65536 | tf_op jit(solution)/shard_map/while/body/eval_jaxpr/psum | solution.py:63
  159.0 7.8 %convolution_subtract_fusion.2 = f32[64,16384]{1,0:T(8,128)S(1)} fusion(f32[128,64]{0,1:T(8,128)S(1)} %broadcast_divide_fusion.4, f32[128,16384]{1,0:T(8,128)} %copy-done, f32[2,64,16384]{2,1,0:T(8,128)} %get-tuple-element.126, s32[]{:T(128)} %get-tuple-element.116, f32[16384]{0:T(1024)S(1)} %fusion.152), kind=kOutput, calls=%fused_computation.1.clone.1 | convolution fusion | flops 1612709888 | bytes 16875524 | tf_op jit(solution)/shard_map/while/body/eval_jaxpr/dot_general | solution.py:27
  172.2 25.3 %psum.28 = f32[64,64]{0,1:T(8,128)S(1)} all-reduce(f32[64,64]{0,1:T(8,128)S(1)} %fusion.154), channel_id=1, replica_groups=mesh['grp'=8,'dev'=16] {'grp'}, use_global_device_ids=true, to_apply=%region_3.3 | all-reduce | flops 4096 | bytes 32768 | tf_op jit(solution)/shard_map/while/body/eval_jaxpr/psum | solution.py:65
  197.6 71.4 %psum.29 = f32[64,64]{0,1:T(8,128)S(1)} all-reduce(f32[64,64]{0,1:T(8,128)S(1)} %psum.28), channel_id=1, replica_groups=mesh['grp'=8,'dev'=16] {'dev'}, use_global_device_ids=true, to_apply=%region_4.4 | all-reduce | flops 4096 | bytes 32768 | tf_op jit(solution)/shard_map/while/body/eval_jaxpr/psum | solution.py:65
  269.1 5.8 cholesky.285
  277.7 11.7 %cholesky.286 = f32[128,128]{1,0:T(8,128)S(1)} custom-call(f32[128,128]{1,0:T(8,128)S(1)} %fusion.160), custom_call_target="Cholesky" | custom-call | tf_op jit(solution)/shard_map/while/body/eval_jaxpr/jit(cholesky)/cholesky | solution.py:48
  290.8 9.8 %custom-call.22 = f32[1,128,128]{1,2,0:T(8,128)S(1)} custom-call(f32[1,128,128]{2,1,0:T(8,128)S(1)} %fusion.162), custom_call_target="InvertDiagBlocksLowerTriangular" | custom-call | tf_op jit(solution)/shard_map/while/body/eval_jaxpr/jit(_solve_triangular)/triangular_solve | solution.py:49
  302.3 11.9 %cholesky.287 = f32[128,128]{1,0:T(8,128)S(1)} custom-call(f32[128,128]{1,0:T(8,128)S(1)} %fusion.167), custom_call_target="Cholesky" | custom-call | tf_op jit(solution)/shard_map/while/body/eval_jaxpr/jit(cholesky)/cholesky | solution.py:48
  315.6 9.8 %custom-call.23 = f32[1,128,128]{1,2,0:T(8,128)S(1)} custom-call(f32[1,128,128]{2,1,0:T(8,128)S(1)} %fusion.169), custom_call_target="InvertDiagBlocksLowerTriangular" | custom-call | tf_op jit(solution)/shard_map/while/body/eval_jaxpr/jit(_solve_triangular)/triangular_solve | solution.py:49
  327.1 11.7 %cholesky.288 = f32[128,128]{1,0:T(8,128)S(1)} custom-call(f32[128,128]{1,0:T(8,128)S(1)} %fusion.174), custom_call_target="Cholesky" | custom-call | tf_op jit(solution)/shard_map/while/body/eval_jaxpr/jit(cholesky)/cholesky | solution.py:48
  340.2 9.8 %custom-call.24 = f32[1,128,128]{1,2,0:T(8,128)S(1)} custom-call(f32[1,128,128]{2,1,0:T(8,128)S(1)} %fusion.175), custom_call_target="InvertDiagBlocksLowerTriangular" | custom-call | tf_op jit(solution)/shard_map/while/body/eval_jaxpr/jit(_solve_triangular)/triangular_solve | solution.py:49
  350.8 4.9 custom-call.25
  355.7 5.6 fusion.177
  361.3 12.3 %fusion.178 = f32[128,16384]{1,0:T(8,128)} fusion(f32[128,192]{0,1:T(8,128)S(1)} %fusion.176, f32[64,16384]{1,0:T(8,128)S(1)} %fusion.177, f32[128,16384]{1,0:T(8,128)} %copy-done), kind=kOutput, calls=%fused_computation.2.clone.1 | convolution fusion | flops 4834983936 | bytes 21069824 | tf_op jit(solution)/shard_map/while/body/eval_jaxpr/dot_general | solution.py:27
  382.7 8.8 %fusion.153 = f32[128,64]{0,1:T(8,128)S(1)} fusion(f32[128,16384]{1,0:T(8,128)S(1)} %copy.45, f32[2,64,16384]{2,1,0:T(8,128)S(1)} %copy-done.2, s32[]{:T(128)} %get-tuple-element.116, f32[16384]{0:T(1024)S(1)} %fusion.152), kind=kOutput, calls=%fused_computation.11.clone.1 | convolution fusion | flops 1611661312 | bytes 12681220 | tf_op jit(solution)/shard_map/while/body/eval_jaxpr/dot_general | solution.py:17
  391.4 63.1 %psum.27 = f32[128,64]{0,1:T(8,128)S(1)} all-reduce(f32[128,64]{0,1:T(8,128)S(1)} %fusion.153), channel_id=1, replica_groups=mesh['grp'=8,'dev'=16] {'grp','dev'}, use_global_device_ids=true, to_apply=%region_2.2 | all-reduce | flops 8192 | bytes 65536 | tf_op jit(solution)/shard_map/while/body/eval_jaxpr/psum | solution.py:63
  454.6 7.8 %convolution_subtract_fusion.2 = f32[64,16384]{1,0:T(8,128)S(1)} fusion(f32[128,64]{0,1:T(8,128)S(1)} %broadcast_divide_fusion.4, f32[128,16384]{1,0:T(8,128)} %copy-done, f32[2,64,16384]{2,1,0:T(8,128)} %get-tuple-element.126, s32[]{:T(128)} %get-tuple-element.116, f32[16384]{0:T(1024)S(1)} %fusion.152), kind=kOutput, calls=%fused_computation.1.clone.1 | convolution fusion | flops 1612709888 | bytes 16875524 | tf_op jit(solution)/shard_map/while/body/eval_jaxpr/dot_general | solution.py:27
  467.8 23.6 %psum.28 = f32[64,64]{0,1:T(8,128)S(1)} all-reduce(f32[64,64]{0,1:T(8,128)S(1)} %fusion.154), channel_id=1, replica_groups=mesh['grp'=8,'dev'=16] {'grp'}, use_global_device_ids=true, to_apply=%region_3.3 | all-reduce | flops 4096 | bytes 32768 | tf_op jit(solution)/shard_map/while/body/eval_jaxpr/psum | solution.py:65
  491.4 71.7 %psum.29 = f32[64,64]{0,1:T(8,128)S(1)} all-reduce(f32[64,64]{0,1:T(8,128)S(1)} %psum.28), channel_id=1, replica_groups=mesh['grp'=8,'dev'=16] {'dev'}, use_global_device_ids=true, to_apply=%region_4.4 | all-reduce | flops 4096 | bytes 32768 | tf_op jit(solution)/shard_map/while/body/eval_jaxpr/psum | solution.py:65
  563.3 5.8 cholesky.285
  571.9 11.7 %cholesky.286 = f32[128,128]{1,0:T(8,128)S(1)} custom-call(f32[128,128]{1,0:T(8,128)S(1)} %fusion.160), custom_call_target="Cholesky" | custom-call | tf_op jit(solution)/shard_map/while/body/eval_jaxpr/jit(cholesky)/cholesky | solution.py:48
  585.0 9.8 %custom-call.22 = f32[1,128,128]{1,2,0:T(8,128)S(1)} custom-call(f32[1,128,128]{2,1,0:T(8,128)S(1)} %fusion.162), custom_call_target="InvertDiagBlocksLowerTriangular" | custom-call | tf_op jit(solution)/shard_map/while/body/eval_jaxpr/jit(_solve_triangular)/triangular_solve | solution.py:49
  596.5 11.9 %cholesky.287 = f32[128,128]{1,0:T(8,128)S(1)} custom-call(f32[128,128]{1,0:T(8,128)S(1)} %fusion.167), custom_call_target="Cholesky" | custom-call | tf_op jit(solution)/shard_map/while/body/eval_jaxpr/jit(cholesky)/cholesky | solution.py:48
  609.8 9.8 %custom-call.23 = f32[1,128,128]{1,2,0:T(8,128)S(1)} custom-call(f32[1,128,128]{2,1,0:T(8,128)S(1)} %fusion.169), custom_call_target="InvertDiagBlocksLowerTriangular" | custom-call | tf_op jit(solution)/shard_map/while/body/eval_jaxpr/jit(_solve_triangular)/triangular_solve | solution.py:49
  621.3 11.7 %cholesky.288 = f32[128,128]{1,0:T(8,128)S(1)} custom-call(f32[128,128]{1,0:T(8,128)S(1)} %fusion.174), custom_call_target="Cholesky" | custom-call | tf_op jit(solution)/shard_map/while/body/eval_jaxpr/jit(cholesky)/cholesky | solution.py:48
  634.4 9.8 %custom-call.24 = f32[1,128,128]{1,2,0:T(8,128)S(1)} custom-call(f32[1,128,128]{2,1,0:T(8,128)S(1)} %fusion.175), custom_call_target="InvertDiagBlocksLowerTriangular" | custom-call | tf_op jit(solution)/shard_map/while/body/eval_jaxpr/jit(_solve_triangular)/triangular_solve | solution.py:49
  649.9 5.8 fusion.177
  655.7 12.3 %fusion.178 = f32[128,16384]{1,0:T(8,128)} fusion(f32[128,192]{0,1:T(8,128)S(1)} %fusion.176, f32[64,16384]{1,0:T(8,128)S(1)} %fusion.177, f32[128,16384]{1,0:T(8,128)} %copy-done), kind=kOutput, calls=%fused_computation.2.clone.1 | convolution fusion | flops 4834983936 | bytes 21069824 | tf_op jit(solution)/shard_map/while/body/eval_jaxpr/dot_general | solution.py:27
  (104 shorter events, 56.7 us)
Async XLA Ops:
  0.6 77.9 %copy-start.4 = (f32[128]{0:T(128)S(1)}, f32[128]{0:T(128)}, u32[]{:S(2)}) copy-start(f32[128]{0:T(128)} %param.10) | copy-start | bytes 1540
  78.8 8.8 %copy-start.2 = (f32[2,64,16384]{2,1,0:T(8,128)S(1)}, f32[2,64,16384]{2,1,0:T(8,128)}, u32[]{:S(2)}) copy-start(f32[2,64,16384]{2,1,0:T(8,128)} %get-tuple-element.126) | copy-start | bytes 25165828 | tf_op jit(solution)/shard_map/while
  82.4 4.3 copy-start
  166.8 2.0 copy-start.1
  373.9 8.8 %copy-start.2 = (f32[2,64,16384]{2,1,0:T(8,128)S(1)}, f32[2,64,16384]{2,1,0:T(8,128)}, u32[]{:S(2)}) copy-start(f32[2,64,16384]{2,1,0:T(8,128)} %get-tuple-element.126) | copy-start | bytes 25165828 | tf_op jit(solution)/shard_map/while
  377.4 4.3 copy-start
  462.4 2.0 copy-start.1
  669.0 0.5 copy-start.3
